TPU v7x, 128 devices: a whole 4x4x4 slice. The times are simulated.
128 devices in a mesh: context: 8 (over z, core), tensor: 16 (over x, y).
Axes of the slice: x: 4, y: 4, z: 4, core: 2. Of those that a mesh axis runs over, the one named last changes fastest.
Arguments:
- features: bfloat16 [4096, 3, 8192], P('context', None, 'tensor'), may hold values from -6 to 6
- se_filter: float32 [7, 3, 8192], P(None, None, 'tensor'), may hold values from -1.6 to 1.6
- mr_filter: bfloat16 [128, 512], P(None, 'tensor'), may hold values from -0.61 to 0.61
- stream: bfloat16 [4096, 8192], P('context', 'tensor'), may hold values from -20 to 20
- w_out: bfloat16 [8192, 8192], P('tensor'), may hold values from -0.09375 to 0.09375
- norm_gain: float32 [8192], replicated, may hold values from 0.1 to 1.9
- w_qkv: bfloat16 [8192, 3, 4096], P(None, None, 'tensor'), as said below
Outputs:
- stream_out: bfloat16 [4096, 8192], P('context', 'tensor')
- context_out: bfloat16 [4096, 4096], P('context', 'tensor')
Inputs may be any that keep to these rules, and one draw needn't show every extreme that they name: `w_qkv`: projection weights.
All inputs are finite; a program needn't handle non-finite values.
Results may differ from a plain program's by a relative error of at most 0.019.
Values may be sent and summed in bfloat16 or wider, within the bound.
No kernel may reach another device: no remote copies, remote signals or barrier semaphores. Data moves between devices by JAX's collectives and lax.ppermute only.
A program may use at most 192 MiB of HBM per device.

v0:
```python
import jax
import jax.numpy as jnp
from jax import lax
from jax.sharding import PartitionSpec as P

HD = 128


def passed_along(value, axis, steps):
    count = lax.axis_size(axis)
    initial, last = (max(0, -steps), min(count, count - steps))
    return lax.ppermute(value, axis, [(source, source + steps) for source in range(initial, last)])


def short_filter(padded, se_filter, row_count):
    se_width = se_filter.shape[0]
    filtered = se_filter[0][None] * padded[se_width - 1 : se_width - 1 + row_count].astype(
        jnp.float32
    )
    for offset_lag in range(1, se_width):
        window = padded[se_width - 1 - offset_lag : se_width - 1 - offset_lag + row_count].astype(
            jnp.float32
        )
        filtered = filtered + se_filter[offset_lag][None] * window
    return filtered


def toeplitz_blocks(mr_filter):
    blocks = mr_filter.shape[0]
    groups = mr_filter.shape[1]
    reversed_taps = mr_filter[::-1].T
    period_row = jnp.concatenate([reversed_taps, jnp.zeros((groups, blocks), jnp.bfloat16)], axis=1)
    tiled = jnp.tile(period_row, (1, blocks))[:, : blocks * (2 * blocks - 1)]
    tiled = tiled.reshape(groups, blocks, 2 * blocks - 1)
    return jnp.concatenate([tiled, jnp.zeros((groups, blocks, 1), jnp.bfloat16)], axis=2)


def medium_filter(kv_prev, kv_prod, mr_filter):
    tok_rows, own_chans = kv_prod.shape
    blocks = mr_filter.shape[0]
    groups = mr_filter.shape[1]
    group_width = own_chans // groups
    block_count = tok_rows // blocks
    extended = jnp.concatenate([kv_prev, kv_prod, jnp.zeros((1, own_chans), jnp.bfloat16)], axis=0)
    lower = extended[:tok_rows].reshape(block_count, blocks, groups, group_width)
    upper = extended[blocks : blocks + tok_rows].reshape(block_count, blocks, groups, group_width)
    toeplitz = toeplitz_blocks(mr_filter)
    medium = jnp.einsum(
        "gim,bmgc->bigc", toeplitz[:, :, :blocks], lower, preferred_element_type=jnp.float32
    )
    medium = medium + jnp.einsum(
        "gim,bmgc->bigc", toeplitz[:, :, blocks:], upper, preferred_element_type=jnp.float32
    )
    return medium.reshape(tok_rows, own_chans)


def on_device(features, se_filter, mr_filter, stream, w_out, norm_gain, w_qkv):
    tok_rows = features.shape[0]
    own_chans = features.shape[2]
    se_width = se_filter.shape[0]
    mr_width = mr_filter.shape[0]
    edge_rows = passed_along(features[tok_rows - (se_width - 1) :], "context", 1)
    short_out = short_filter(jnp.concatenate([edge_rows, features], axis=0), se_filter, tok_rows)
    kv_prod = (short_out[:, 1, :] * short_out[:, 2, :]).astype(jnp.bfloat16)
    kv_prev = passed_along(kv_prod[tok_rows - (mr_width - 1) :], "context", 1)
    medium = medium_filter(kv_prev, kv_prod, mr_filter)
    gated = (short_out[:, 0, :] * medium).astype(jnp.bfloat16)
    tensor_rank = lax.axis_index("tensor")
    partial_value = jnp.dot(gated, w_out, preferred_element_type=jnp.float32)
    own_cols = lax.dynamic_slice_in_dim(
        partial_value, tensor_rank * own_chans, own_chans, 1
    ) + stream.astype(jnp.float32)
    term_all = lax.dynamic_update_slice_in_dim(partial_value, own_cols, tensor_rank * own_chans, 1)
    mixed_rows = lax.psum(term_all, "tensor")
    stream_out = lax.dynamic_slice_in_dim(mixed_rows, tensor_rank * own_chans, own_chans, 1).astype(
        jnp.bfloat16
    )
    mean_square = jnp.mean(mixed_rows * mixed_rows, axis=1, keepdims=True)
    normed = (mixed_rows * lax.rsqrt(mean_square + 1e-05) * norm_gain[None, :]).astype(jnp.bfloat16)
    qkv_proj = jnp.einsum("td,dkh->tkh", normed, w_qkv, preferred_element_type=jnp.float32).astype(
        jnp.bfloat16
    )
    head_cols = w_qkv.shape[2]
    head_count = head_cols // HD
    query = qkv_proj[:, 0, :].reshape(tok_rows, head_count, HD)
    position = lax.axis_index("context") * tok_rows + jnp.arange(tok_rows, dtype=jnp.int32)
    scale_factor = HD ** (-0.5)
    run_max = jnp.full((head_count, tok_rows), -1e30, jnp.float32)
    key_block = lax.all_gather(qkv_proj[:, 1, :], "context", axis=0, tiled=True)
    value_block = lax.all_gather(qkv_proj[:, 2, :], "context", axis=0, tiled=True)
    key_count = key_block.shape[0]
    keys_three = key_block.reshape(key_count, head_count, HD)
    values_three = value_block.reshape(key_count, head_count, HD)
    scores = (
        jnp.einsum("qhd,khd->hqk", query, keys_three, preferred_element_type=jnp.float32)
        * scale_factor
    )
    key_position = jnp.arange(key_count, dtype=jnp.int32)
    allowed = key_position[None, :] <= position[:, None]
    scores = jnp.where(allowed[None], scores, -jnp.inf)
    new_max = jnp.maximum(run_max, jnp.max(scores, axis=2))
    expo = jnp.exp(scores - new_max[:, :, None])
    run_total = jnp.sum(expo, axis=2)
    weights = expo.astype(jnp.bfloat16)
    run_acc = jnp.einsum("hqk,khd->hqd", weights, values_three, preferred_element_type=jnp.float32)
    run_max, run_total, run_acc = (new_max, run_total, run_acc)
    result = run_acc / run_total[:, :, None]
    context_out = jnp.transpose(result, (1, 0, 2)).reshape(tok_rows, head_cols).astype(jnp.bfloat16)
    return (stream_out, context_out)


def solution(mesh):
    placed = (
        P("context", None, "tensor"),
        P(None, None, "tensor"),
        P(None, "tensor"),
        P("context", "tensor"),
        P("tensor", None),
        P(),
        P(None, None, "tensor"),
    )
    return jax.shard_map(
        on_device,
        mesh=mesh,
        in_specs=placed,
        out_specs=(P("context", "tensor"), P("context", "tensor")),
        check_vma=False,
    )
```

profile of v0, /device:TPU:1, one launch (start us, length us, event | category | flops | bytes accessed | tf_op | source)
XLA Modules:
  0.0 383.0 jit_solution(14725790758552800340)
XLA Ops:
  8.2 4.9 %collective-permute-start = (bf16[6,3,512]{0,2,1:T(8,128)(2,1)S(1)}, bf16[6,3,512]{0,2,1:T(8,128)(2,1)S(1)}, u32[]{:S(2)}, u32[]{:S(2)}) collective-permute-start(bf16[6,3,512]{0,2,1:T(8,128)(2,1)S(1)} %copy.14), channel_id=1, source_target_pairs={{0,16},{16,32},{32,48},{48,64},{64,80},{80,96},{96,112},{1,17},{17... | collective-permute-start | bytes 55304 | tf_op jit(solution)/shard_map/ppermute | solution.py:12
  15.6 2.6 copy.13
  18.5 1.2 copy.35
  19.8 7.8 %reshape.68 = bf16[32,128,255]{2,1,0:T(8,128)(2,1)} reshape(bf16[32,32640]{1,0:T(8,128)(2,1)S(1)} %slice.124) | data formatting | bytes 4177920 | tf_op jit(solution)/shard_map/reshape | solution.py:34
  28.2 12.6 %multiply_add_fusion = f32[512,3,512]{0,2,1:T(8,128)S(1)} fusion(bf16[512,3,512]{0,2,1:T(8,128)(2,1)} %copy.13, bf16[6,3,512]{0,2,1:T(8,128)(2,1)S(1)} %collective-permute-done, f32[3,512]{1,0:T(4,128)S(1)} %get-tuple-element.20, f32[3,512]{1,0:T(4,128)S(1)} %get-tuple-element.21, f32[3,512]{1,0:T(4,128)} %get-tuple-element.22, ...), kind=kLoop, calls=%fused_computation.19 | loop fusion | flops 29884416 | bytes 4780032 | tf_op jit(solution)/shard_map/add | solution.py:24
  41.1 1.9 collective-permute-start.1
  43.2 1.8 collective-permute-done.1
  44.9 1.5 pad_maximum_fusion.1
  46.4 2.0 reshape.69
  48.4 2.0 reshape.67
  50.4 2.3 fusion.24
  54.0 11.6 %fusion.34 = f32[512,8192]{1,0:T(8,128)} fusion(bf16[512,8192]{1,0:T(8,128)(2,1)} %param.11, f32[64,8,4,128]{3,2,1,0:T(4,128)S(1)} %bitcast.73, f32[512,3,512]{0,2,1:T(8,128)S(1)} %multiply_add_fusion), kind=kOutput, calls=%fused_computation.49 | convolution fusion | flops 4295491584 | bytes 27262976 | tf_op jit(solution)/shard_map/dot_general | solution.py:69
  65.6 2.4 add_dynamic-update-slice_fusion
  68.2 222.7 %all-reduce.5.cloned.1.call-done = f32[512,8192]{1,0:T(8,128)} async-done(((f32[512,8192]{1,0:T(8,128)}), f32[512,8192]{1,0:T(8,128)}) %all-reduce.5.cloned.1.call-update) | async-done | bytes 16777232 | tf_op jit(solution)/shard_map/psum | solution.py:74
  290.9 7.0 %multiply_reduce_fusion = f32[512]{0:T(512)S(1)} fusion(f32[512,8192]{1,0:T(8,128)} %all-reduce.5.cloned.1.call-done), kind=kLoop, calls=%fused_computation.3 | loop fusion | flops 8388096 | bytes 16779264 | tf_op jit(solution)/shard_map/reduce_sum | solution.py:78
  297.9 14.8 %fusion.16 = bf16[512,3,256]{0,2,1:T(8,128)(2,1)S(1)} fusion(bf16[8192,3,256]{2,0,1:T(8,128)(2,1)} %param.13, f32[512,8192]{1,0:T(8,128)} %all-reduce.5.cloned.1.call-done, f32[8192]{0:T(1024)S(1)} %copy-done.5, f32[512]{0:T(512)S(1)} %add_rsqrt_fusion), kind=kOutput, calls=%fused_computation.32 | convolution fusion | flops 6455427072 | bytes 30181376 | tf_op jit(solution)/shard_map/td,dkh->tkh/dot_general | solution.py:80
  314.3 1.7 iota_compare_fusion
  316.0 2.1 dynamic-slice_convert_fusion
  318.1 21.7 %all-gather.5.cloned.1.call-done = bf16[4096,1,256]{0,2,1:T(8,128)(2,1)} async-done(((bf16[512,1,256]{0,2,1:T(8,128)(2,1)}), bf16[4096,1,256]{0,2,1:T(8,128)(2,1)}) %all-gather.5.cloned.1.call-update) | async-done | bytes 2097168 | tf_op jit(solution)/shard_map/all_gather | solution.py:89
  339.7 5.3 %fusion = (f32[2,512]{1,0:T(2,128)S(1)}, f32[2,512,4096]{2,1,0:T(8,128)S(1)}) fusion(pred[512,4096]{1,0:T(8,128)(4,1)S(1)} %iota_compare_fusion, bf16[512,2,128]{0,2,1:T(8,128)(2,1)S(1)} %bitcast.77, bf16[4096,2,128]{0,2,1:T(8,128)(2,1)} %bitcast.81), kind=kOutput, calls=%fused_computation.4 | convolution fusion | flops 1086323712 | bytes 21237760 | tf_op jit(solution)/shard_map/qhd,khd->hqk/dot_general | solution.py:95
  345.1 5.7 %copy-done = f32[2,512,4096]{2,1,0:T(8,128)} copy-done((f32[2,512,4096]{2,1,0:T(8,128)}, f32[2,512,4096]{2,1,0:T(8,128)S(1)}, u32[]{:S(2)}) %copy-start) | copy-done | bytes 16777240
  350.8 4.6 %fusion.1 = f32[2,512]{1,0:T(2,128)S(1)} fusion(f32[2,512,4096]{2,1,0:T(8,128)S(1)} %get-tuple-element.19, f32[2,512]{1,0:T(2,128)S(1)} %broadcast_maximum_fusion, pred[512,4096]{1,0:T(8,128)(4,1)S(1)} %iota_compare_fusion), kind=kLoop, calls=%fused_computation.5 | loop fusion | flops 16776192 | bytes 18882560 | tf_op jit(solution)/shard_map/reduce_sum | solution.py:103
  355.4 11.9 %all-gather.7.cloned.1.call-done = bf16[4096,1,256]{0,2,1:T(8,128)(2,1)} async-done(((bf16[512,1,256]{0,2,1:T(8,128)(2,1)}), bf16[4096,1,256]{0,2,1:T(8,128)(2,1)}) %all-gather.7.cloned.1.call-update) | async-done | bytes 2097168 | tf_op jit(solution)/shard_map/all_gather | solution.py:90
  367.2 8.4 %fusion.31 = bf16[512,2,128]{0,2,1:T(8,128)(2,1)S(1)} fusion(bf16[4096,2,128]{0,2,1:T(8,128)(2,1)} %bitcast.82, f32[2,512,4096]{2,1,0:T(8,128)} %copy-done, f32[2,512]{1,0:T(2,128)S(1)} %broadcast_maximum_fusion, pred[512,4096]{1,0:T(8,128)(4,1)S(1)} %iota_compare_fusion, f32[512,2]{0,1:T(2,128)S(1)} %bitcast.80), kind=kOutput, calls=%fused_computation.47 | convolution fusion | flops 1090781184 | bytes 21241856 | tf_op jit(solution)/shard_map/hqk,khd->hqd/dot_general | solution.py:105
  (39 shorter events, 8.8 us)
Async XLA Ops:
  7.2 11.1 %copy-start.4 = (bf16[128,32]{0,1:T(8,128)(2,1)S(1)}, bf16[128,32]{0,1:T(8,128)(2,1)}, u32[]{:S(2)}) copy-start(bf16[128,32]{0,1:T(8,128)(2,1)} %param.9) | copy-start | bytes 24580
  7.2 283.8 %all-reduce.5.cloned.1.call-start = ((), (), s32[]{:S(2)}) async-start(), calls=%async_computation | async-start | bytes 33554432 | tf_op jit(solution)/shard_map/psum | solution.py:74
  8.2 20.0 %collective-permute-start = (bf16[6,3,512]{0,2,1:T(8,128)(2,1)S(1)}, bf16[6,3,512]{0,2,1:T(8,128)(2,1)S(1)}, u32[]{:S(2)}, u32[]{:S(2)}) collective-permute-start(bf16[6,3,512]{0,2,1:T(8,128)(2,1)S(1)} %copy.14), channel_id=1, source_target_pairs={{0,16},{16,32},{32,48},{48,64},{64,80},{80,96},{96,112},{1,17},{17... | collective-permute-start | bytes 55304 | tf_op jit(solution)/shard_map/ppermute | solution.py:12
  41.1 3.9 %collective-permute-start.1 = (bf16[127,512]{0,1:T(8,128)(2,1)S(1)}, bf16[127,512]{0,1:T(8,128)(2,1)S(1)}, u32[]{:S(2)}, u32[]{:S(2)}) collective-permute-start(bf16[127,512]{0,1:T(8,128)(2,1)S(1)} %slice_bitcast_fusion.3), channel_id=1, source_target_pairs={{0,16},{16,32},{32,48},{48,64},{64,80},{80,96},{96,112},{1,17},{17... | collective-permute-start | bytes 390152 | tf_op jit(solution)/shard_map/ppermute | solution.py:12
  50.4 2.3 copy-start.1
  50.4 2.4 copy-start.2
  54.0 11.6 %copy-start.3 = (bf16[512,512]{1,0:T(8,128)(2,1)S(1)}, bf16[512,512]{1,0:T(8,128)(2,1)}, u32[]{:S(2)}) copy-start(bf16[512,512]{1,0:T(8,128)(2,1)} %param.10) | copy-start | bytes 1572868
  68.0 229.9 %copy-start.5 = (f32[8192]{0:T(1024)S(1)}, f32[8192]{0:T(1024)}, u32[]{:S(2)}) copy-start(f32[8192]{0:T(1024)} %param.12) | copy-start | bytes 98308
  68.0 271.8 %all-gather.5.cloned.1.call-start = ((), (), s32[]{:S(2)}) async-start(), calls=%async_computation.1 | async-start | bytes 2359296 | tf_op jit(solution)/shard_map/all_gather | solution.py:89
  313.6 53.7 %all-gather.7.cloned.1.call-start = ((), (), s32[]{:S(2)}) async-start(), calls=%async_computation.2 | async-start | bytes 2359296 | tf_op jit(solution)/shard_map/all_gather | solution.py:90
  345.0 5.7 %copy-start = (f32[2,512,4096]{2,1,0:T(8,128)}, f32[2,512,4096]{2,1,0:T(8,128)S(1)}, u32[]{:S(2)}) copy-start(f32[2,512,4096]{2,1,0:T(8,128)S(1)} %get-tuple-element.19) | copy-start | bytes 50331652
Sparse Core Ops, SparseCore 0:
  68.1 222.7 all-reduce.4
  313.7 26.0 all-gather.4
  341.4 25.7 all-gather.6
where the time goes:
time: 384 us; the launch traced here: 383 us
  waiting for transfers between devices  259 us (67%)
  matrix products  43.2 us (11%)
  local copies, waits for them, and re-layouts  30 us (8%)
  other arithmetic  30 us (8%)
  between operations  13.9 us (4%)
  starting transfers between devices  7.16 us (2%)
    psum x1, waiting for transfers between devices, on_device(): mixed_rows = lax.psum(term_all, 'tensor')  223 us
    all_gather x1, waiting for transfers between devices, on_device(): key_block = lax.all_gather(qkv_proj[:, 1, :], 'context', axis=0, tiled=True)  21.7 us
    dot_general x1, matrix products, on_device(): jnp.einsum('td,dkh->tkh', normed, w_qkv, preferred_element_type=jnp.float32)  14.8 us
    add x1, other arithmetic, short_filter(): filtered = filtered + se_filter[offset_lag][None] * window  12.6 us
    unnamed x19, local copies, waits for them, and re-layouts  12.2 us
    all_gather x1, waiting for transfers between devices, on_device(): lax.all_gather(qkv_proj[:, 2, :], 'context', axis=0, tiled=True)  11.9 us
    dot_general x1, matrix products, on_device(): partial_value = jnp.dot(gated, w_out, preferred_element_type=jnp.float32)  11.6 us
    dot_general x1, matrix products, on_device(): jnp.einsum('hqk,khd->hqd', weights, values_three, preferred_element_type=...  8.42 us
  transfers between devices with their start and end apart: 5, of which 4 were waited for; matrix products, arithmetic and copies ran while one was open for 8% of the time, Pallas kernels for 0%

commit v1 on v0

--- a/solution.py
+++ b/solution.py
@@ -87,7 +87,10 @@
     scale_factor = HD ** (-0.5)
     run_max = jnp.full((head_count, tok_rows), -1e30, jnp.float32)
     key_block = lax.all_gather(qkv_proj[:, 1, :], "context", axis=0, tiled=True)
-    value_block = lax.all_gather(qkv_proj[:, 2, :], "context", axis=0, tiled=True)
+    value_block = jnp.concatenate(
+        lax.all_to_all(jnp.stack([qkv_proj[:, 2, :]] * lax.axis_size("context")), "context", 0, 0),
+        axis=0,
+    )
     key_count = key_block.shape[0]
     keys_three = key_block.reshape(key_count, head_count, HD)
     values_three = value_block.reshape(key_count, head_count, HD)

time: 384 us -> 389 us (1.013)
  starting transfers between devices: 7.16 us -> 12.6 us
  local copies, waits for them, and re-layouts: 30 us -> 34 us
    all_to_all x0 -> x1, waiting for transfers between devices: none -> 31.1 us  [on_device(): lax.all_to_all(jnp.stack([qkv_proj[:, 2, :]] * lax.axis_size('context')),...]
    all_gather x1, waiting for transfers between devices: 21.7 us -> 0.01 us  [on_device(): key_block = lax.all_gather(qkv_proj[:, 1, :], 'context', axis=0, tiled=True)]
    all_gather x1 -> x0, waiting for transfers between devices: 11.9 us -> none  [on_device(): lax.all_gather(qkv_proj[:, 2, :], 'context', axis=0, tiled=True)]
    unnamed x19 -> x17, local copies, waits for them, and re-layouts: 12.2 us -> 6.5 us
    another operation x0 -> x2, local copies, waits for them, and re-layouts: none -> 5.7 us  [the longest x1 4.19 us: on_device(): values_three = value_block.reshape(key_count, head_count, HD)]
    all_to_all x0 -> x1, starting transfers between devices: none -> 5.51 us  [on_device(): lax.all_to_all(jnp.stack([qkv_proj[:, 2, :]] * lax.axis_size('context')),...]
    all_to_all x0 -> x1, local copies, waits for them, and re-layouts: none -> 4.09 us  [on_device(): lax.all_to_all(jnp.stack([qkv_proj[:, 2, :]] * lax.axis_size('context')),...]
  transfers between devices with their start and end apart: 5 -> 5, of which waited for: 4 -> 3; matrix products, arithmetic and copies ran while one was open for 8% -> 7% of each run, Pallas kernels for 0% -> 0%
where the time goes in v1:
time: 389 us; the launch traced here: 388 us
  waiting for transfers between devices  256 us (66%)
  matrix products  41.6 us (11%)
  local copies, waits for them, and re-layouts  34 us (9%)
  other arithmetic  30 us (8%)
  between operations  14.2 us (4%)
  starting transfers between devices  12.6 us (3%)
    psum x1, waiting for transfers between devices, on_device(): mixed_rows = lax.psum(term_all, 'tensor')  223 us
    all_to_all x1, waiting for transfers between devices, on_device(): lax.all_to_all(jnp.stack([qkv_proj[:, 2, :]] * lax.axis_size('context')),...  31.1 us
    dot_general x1, matrix products, on_device(): jnp.einsum('td,dkh->tkh', normed, w_qkv, preferred_element_type=jnp.float32)  14.8 us
    add x1, other arithmetic, short_filter(): filtered = filtered + se_filter[offset_lag][None] * window  12.6 us
    dot_general x1, matrix products, on_device(): partial_value = jnp.dot(gated, w_out, preferred_element_type=jnp.float32)  11.6 us
    reshape x1, local copies, waits for them, and re-layouts, toeplitz_blocks(): tiled = tiled.reshape(groups, blocks, 2 * blocks - 1)  7.8 us
  transfers between devices with their start and end apart: 5, of which 3 were waited for; matrix products, arithmetic and copies ran while one was open for 7% of the time, Pallas kernels for 0%

profile of v1, /device:TPU:1, one launch (start us, length us, event | category | flops | bytes accessed | tf_op | source)
XLA Modules:
  0.0 387.9 jit_solution(4583615009603778252)
XLA Ops:
  8.2 4.9 %collective-permute-start = (bf16[6,3,512]{0,2,1:T(8,128)(2,1)S(1)}, bf16[6,3,512]{0,2,1:T(8,128)(2,1)S(1)}, u32[]{:S(2)}, u32[]{:S(2)}) collective-permute-start(bf16[6,3,512]{0,2,1:T(8,128)(2,1)S(1)} %copy.24), channel_id=1, source_target_pairs={{0,16},{16,32},{32,48},{48,64},{64,80},{80,96},{96,112},{1,17},{17... | collective-permute-start | bytes 55304 | tf_op jit(solution)/shard_map/ppermute | solution.py:12
  15.6 2.6 copy.23
  19.8 7.8 %reshape.67 = bf16[32,128,255]{2,1,0:T(8,128)(2,1)} reshape(bf16[32,32640]{1,0:T(8,128)(2,1)S(1)} %slice.124) | data formatting | bytes 4177920 | tf_op jit(solution)/shard_map/reshape | solution.py:34
  28.2 12.6 %multiply_add_fusion = f32[512,3,512]{0,2,1:T(8,128)S(1)} fusion(bf16[512,3,512]{0,2,1:T(8,128)(2,1)} %copy.23, bf16[6,3,512]{0,2,1:T(8,128)(2,1)S(1)} %collective-permute-done, f32[3,512]{1,0:T(4,128)S(1)} %get-tuple-element.22, f32[3,512]{1,0:T(4,128)S(1)} %get-tuple-element.23, f32[3,512]{1,0:T(4,128)} %get-tuple-element.24, ...), kind=kLoop, calls=%fused_computation.19 | loop fusion | flops 29884416 | bytes 4780032 | tf_op jit(solution)/shard_map/add | solution.py:24
  41.1 1.9 collective-permute-start.1
  43.2 1.8 collective-permute-done.1
  46.4 2.0 reshape.68
  48.3 2.0 reshape.66
  50.3 2.3 fusion.24
  53.9 11.6 %fusion.34 = f32[512,8192]{1,0:T(8,128)} fusion(bf16[512,8192]{1,0:T(8,128)(2,1)} %param.11, f32[64,8,4,128]{3,2,1,0:T(4,128)S(1)} %bitcast.76, f32[512,3,512]{0,2,1:T(8,128)S(1)} %multiply_add_fusion), kind=kOutput, calls=%fused_computation.49 | convolution fusion | flops 4295491584 | bytes 27262976 | tf_op jit(solution)/shard_map/dot_general | solution.py:69
  65.5 2.4 add_dynamic-update-slice_fusion
  68.2 222.7 %all-reduce.5.cloned.1.call-done = f32[512,8192]{1,0:T(8,128)} async-done(((f32[512,8192]{1,0:T(8,128)}), f32[512,8192]{1,0:T(8,128)}) %all-reduce.5.cloned.1.call-update) | async-done | bytes 16777232 | tf_op jit(solution)/shard_map/psum | solution.py:74
  290.8 7.0 %multiply_reduce_fusion = f32[512]{0:T(512)S(1)} fusion(f32[512,8192]{1,0:T(8,128)} %all-reduce.5.cloned.1.call-done), kind=kLoop, calls=%fused_computation.3 | loop fusion | flops 8388096 | bytes 16779264 | tf_op jit(solution)/shard_map/reduce_sum | solution.py:78
  297.8 14.8 %fusion.16 = bf16[512,3,256]{0,2,1:T(8,128)(2,1)S(1)} fusion(bf16[8192,3,256]{2,0,1:T(8,128)(2,1)} %param.13, f32[512,8192]{1,0:T(8,128)} %all-reduce.5.cloned.1.call-done, f32[8192]{0:T(1024)S(1)} %copy-done.4, f32[512]{0:T(512)S(1)} %add_rsqrt_fusion), kind=kOutput, calls=%fused_computation.32 | convolution fusion | flops 6455427072 | bytes 30181376 | tf_op jit(solution)/shard_map/td,dkh->tkh/dot_general | solution.py:80
  313.4 1.5 stack.3
  314.9 5.5 %all-to-all-start = ((bf16[8,512,256]{1,2,0:T(8,128)(2,1)}), bf16[8,512,256]{1,2,0:T(8,128)(2,1)}, u32[]{:S(2)}, u32[]{:S(2)}) async-start(bf16[8,512,256]{1,2,0:T(8,128)(2,1)} %stack.3), calls=%async_computation | async-start | bytes 4194304 | tf_op jit(solution)/shard_map/all_to_all | solution.py:91
  320.4 1.7 iota_compare_fusion
  322.1 2.1 dynamic-slice_convert_fusion
  324.2 31.1 %all-to-all-done = bf16[8,512,256]{1,2,0:T(8,128)(2,1)} async-done(((bf16[8,512,256]{1,2,0:T(8,128)(2,1)}), bf16[8,512,256]{1,2,0:T(8,128)(2,1)}, u32[]{:S(2)}, u32[]{:S(2)}) %all-to-all-start) | async-done | bytes 2097184 | tf_op jit(solution)/shard_map/all_to_all | solution.py:91
  355.3 4.1 %copy.32 = bf16[8,512,256]{1,0,2:T(8,128)(2,1)} copy(bf16[8,512,256]{1,2,0:T(8,128)(2,1)} %all-to-all-done) | data formatting | bytes 4194304 | tf_op jit(solution)/shard_map/all_to_all | solution.py:91
  359.4 4.2 %reshape_reshape.3 = bf16[4096,2,128]{0,2,1:T(8,128)(2,1)} reshape(bf16[8,512,256]{1,0,2:T(8,128)(2,1)} %copy.32) | data formatting | bytes 4194304 | tf_op jit(solution)/shard_map/reshape;reshape | solution.py:96
  363.6 5.3 %fusion = (f32[2,512]{1,0:T(2,128)S(1)}, f32[2,512,4096]{2,1,0:T(8,128)S(1)}) fusion(pred[512,4096]{1,0:T(8,128)(4,1)S(1)} %iota_compare_fusion, bf16[512,2,128]{0,2,1:T(8,128)(2,1)S(1)} %bitcast.80, bf16[4096,2,128]{0,2,1:T(8,128)(2,1)} %bitcast.84), kind=kOutput, calls=%fused_computation.4 | convolution fusion | flops 1086323712 | bytes 21237760 | tf_op jit(solution)/shard_map/qhd,khd->hqk/dot_general | solution.py:98
  368.9 4.6 %fusion.1 = f32[2,512]{1,0:T(2,128)S(1)} fusion(f32[2,512,4096]{2,1,0:T(8,128)S(1)} %get-tuple-element.21, f32[2,512]{1,0:T(2,128)S(1)} %broadcast_maximum_fusion, pred[512,4096]{1,0:T(8,128)(4,1)S(1)} %iota_compare_fusion), kind=kLoop, calls=%fused_computation.5 | loop fusion | flops 16776192 | bytes 18882560 | tf_op jit(solution)/shard_map/reduce_sum | solution.py:106
  373.6 6.7 %fusion.31 = bf16[512,2,128]{0,2,1:T(8,128)(2,1)S(1)} fusion(bf16[4096,2,128]{0,2,1:T(8,128)(2,1)} %reshape_reshape.3, f32[2,512,4096]{2,1,0:T(8,128)S(1)} %get-tuple-element.21, f32[2,512]{1,0:T(2,128)S(1)} %broadcast_maximum_fusion, pred[512,4096]{1,0:T(8,128)(4,1)S(1)} %iota_compare_fusion, f32[512,2]{0,1:T(2,128)S(1)} %bitcast.83), kind=kOutput, calls=%fused_computation.47 | convolution fusion | flops 1090781184 | bytes 21241856 | tf_op jit(solution)/shard_map/hqk,khd->hqd/dot_general | solution.py:108
  (39 shorter events, 10.7 us)
Async XLA Ops:
  7.2 11.0 %copy-start.3 = (bf16[128,32]{0,1:T(8,128)(2,1)S(1)}, bf16[128,32]{0,1:T(8,128)(2,1)}, u32[]{:S(2)}) copy-start(bf16[128,32]{0,1:T(8,128)(2,1)} %param.9) | copy-start | bytes 24580
  7.2 283.7 %all-reduce.5.cloned.1.call-start = ((), (), s32[]{:S(2)}) async-start(), calls=%async_computation.1 | async-start | bytes 33554432 | tf_op jit(solution)/shard_map/psum | solution.py:74
  8.2 20.0 %collective-permute-start = (bf16[6,3,512]{0,2,1:T(8,128)(2,1)S(1)}, bf16[6,3,512]{0,2,1:T(8,128)(2,1)S(1)}, u32[]{:S(2)}, u32[]{:S(2)}) collective-permute-start(bf16[6,3,512]{0,2,1:T(8,128)(2,1)S(1)} %copy.24), channel_id=1, source_target_pairs={{0,16},{16,32},{32,48},{48,64},{64,80},{80,96},{96,112},{1,17},{17... | collective-permute-start | bytes 55304 | tf_op jit(solution)/shard_map/ppermute | solution.py:12
  41.1 3.9 collective-permute-start.1
  50.3 2.3 copy-start
  50.3 2.4 copy-start.1
  53.9 11.6 %copy-start.2 = (bf16[512,512]{1,0:T(8,128)(2,1)S(1)}, bf16[512,512]{1,0:T(8,128)(2,1)}, u32[]{:S(2)}) copy-start(bf16[512,512]{1,0:T(8,128)(2,1)} %param.10) | copy-start | bytes 1572868
  67.9 229.9 %copy-start.4 = (f32[8192]{0:T(1024)S(1)}, f32[8192]{0:T(1024)}, u32[]{:S(2)}) copy-start(f32[8192]{0:T(1024)} %param.12) | copy-start | bytes 98308
  67.9 295.6 %all-gather.3.cloned.1.call-start = ((), (), s32[]{:S(2)}) async-start(), calls=%async_computation.2 | async-start | bytes 2359296 | tf_op jit(solution)/shard_map/all_gather | solution.py:89
  314.9 40.4 %all-to-all-start = ((bf16[8,512,256]{1,2,0:T(8,128)(2,1)}), bf16[8,512,256]{1,2,0:T(8,128)(2,1)}, u32[]{:S(2)}, u32[]{:S(2)}) async-start(bf16[8,512,256]{1,2,0:T(8,128)(2,1)} %stack.3), calls=%async_computation | async-start | bytes 4194304 | tf_op jit(solution)/shard_map/all_to_all | solution.py:91
Sparse Core Ops, SparseCore 0:
  68.1 222.7 all-reduce.4
  313.5 34.7 all-gather.2
